TPU v7x, 512 devices: a whole 4x4x16 slice. The times are simulated.
512 devices in a mesh: tm: 64 (over y, z), rows: 8 (over x, core).
Axes of the slice: x: 4, y: 4, z: 16, core: 2. Of those that a mesh axis runs over, the one named last changes fastest.
Arguments:
- states: float32 [128, 64, 640], P('tm'), may hold values from -6 to 6
- ancestors: int32 [128, 640], P('tm'), may hold values from 0 to 639
- tracer_obs: float32 [128, 32], P('tm'), may hold values from -6 to 6
- jitter: float32 [128], P('tm'), may hold values from 0.00390625 to 0.0390625
- fingerprints: float32 [64, 32], replicated, may hold values from -0.75 to 0.75
- tracer_scale: float32 [32], replicated, may hold values from 0.15 to 0.45
- prior_weights: float32 [640], replicated, may hold values from 0.25 to 4
Outputs:
- filtered: float32 [128, 640], P('tm', 'rows')
All inputs are finite; a program needn't handle non-finite values.
Results may differ from a plain program's by a relative error of at most 0.0003.
Values sent between devices are 32-bit elements; how exact they have to be, the bound alone decides.
A program may use at most 64 MiB of HBM per device.

v0:
```python
import jax
import jax.numpy as jnp
from jax import lax
from jax.sharding import PartitionSpec as P


def shifted(block, axis, distance):
    devices = range(lax.axis_size(axis))
    route = [(i - distance, i) for i in devices if i - distance in devices]
    return lax.ppermute(block, axis, route)


def transition(previous, current, parent_ids, observed, mixing, fingerprints, tracer_scale):
    count = current.shape[1]
    highest = lax.Precision.HIGHEST
    inner_prod = lax.dot_general(
        previous,
        current,
        (((0,), (0,)), ((), ())),
        precision=highest,
        preferred_element_type=jnp.float32,
    )
    distance = (
        jnp.sum(previous * previous, axis=0)[:, None]
        + jnp.sum(current * current, axis=0)[None, :]
        - 2.0 * inner_prod
    )
    kernel = jnp.exp(-2.0 * distance / current.shape[0])
    predicted = lax.dot_general(
        fingerprints,
        current,
        (((0,), (0,)), ((), ())),
        precision=highest,
        preferred_element_type=jnp.float32,
    )
    misfit = tracer_scale[:, None] * (observed[:, None] - predicted)
    likelihood = jnp.exp(-0.5 * jnp.sum(misfit * misfit, axis=0))
    parent = (parent_ids[None, :] == jnp.arange(count, dtype=jnp.int32)[:, None]).astype(
        jnp.float32
    )
    weight = likelihood[None, :] * (parent + mixing * kernel)
    return weight * (count / jnp.sum(weight))


def shards(states, ancestors, tracer_obs, jitter, fingerprints, tracer_scale, prior_weights):
    highest = lax.Precision.HIGHEST
    count = states.shape[2]
    own_rows = count // lax.axis_size("rows")
    row_start = lax.axis_index("rows") * own_rows
    time_index = lax.axis_index("tm")
    rim = shifted(states[-1], "tm", 1)
    local_ids = row_start + lax.broadcasted_iota(jnp.int32, (own_rows, count), 0)
    column_ids = lax.broadcasted_iota(jnp.int32, (own_rows, count), 1)
    block_init = (local_ids == column_ids).astype(jnp.float32)

    def accumulate(carry, inputs):
        running, previous = carry
        current, parent_ids, observed, mixing = inputs
        matrix = transition(
            previous, current, parent_ids, observed, mixing, fingerprints, tracer_scale
        )
        running = jnp.dot(running, matrix, precision=highest, preferred_element_type=jnp.float32)
        kept = lax.dynamic_slice_in_dim(matrix, row_start, own_rows, 0)
        return ((running, current), kept)

    (block_part, unused), kept_rows = lax.scan(
        accumulate, (block_init, rim), (states, ancestors, tracer_obs, jitter)
    )
    full_block = lax.all_gather(block_part, "rows", axis=0, tiled=True)
    start = prior_weights / jnp.sum(prior_weights)

    def turn(turn_index, incoming):
        moved = jnp.dot(incoming, full_block, precision=highest, preferred_element_type=jnp.float32)
        moved = moved / jnp.sum(moved)
        received = shifted(moved, "tm", 1)
        return jnp.where(time_index == 0, start, received)

    incoming = lax.fori_loop(0, lax.axis_size("tm") - 1, turn, start)

    def propagate(weights_now, kept):
        mine = lax.dynamic_slice_in_dim(weights_now, row_start, own_rows, 0)
        partial_term = jnp.dot(mine, kept, precision=highest, preferred_element_type=jnp.float32)
        moved = lax.psum(partial_term, "rows")
        moved = moved / jnp.sum(moved)
        return (moved, count * lax.dynamic_slice_in_dim(moved, row_start, own_rows, 0))

    unused_last, filtered = lax.scan(propagate, incoming, kept_rows)
    return filtered


def solution(mesh):
    return jax.shard_map(
        shards,
        mesh=mesh,
        in_specs=(P("tm", None, None), P("tm", None), P("tm", None), P("tm"), P(), P(), P()),
        out_specs=P("tm", "rows"),
        check_vma=False,
    )
```

profile of v0, /device:TPU:25, one launch (start us, length us, event | category | flops | bytes accessed | tf_op | source)
XLA Modules:
  0.0 808.5 jit_solution(13679982750202817545)
XLA Ops:
  11.1 11.5 %collective-permute-done.1 = f32[64,640]{1,0:T(8,128)S(1)} collective-permute-done((f32[64,640]{1,0:T(8,128)S(1)}, f32[64,640]{1,0:T(8,128)S(1)}, u32[]{:S(2)}, u32[]{:S(2)}) %collective-permute-start.1) | collective-permute-done | bytes 163872 | tf_op jit(solution)/shard_map/ppermute | solution.py:10
  22.7 20.1 %while.42 = (s32[]{:T(128)}, f32[80,640]{1,0:T(8,128)S(1)}, f32[64,640]{1,0:T(8,128)S(1)}, f32[2,80,640]{2,1,0:T(8,128)S(1)}, f32[32]{0:T(128)}, /*index=5*/f32[...) while((s32[]{:T(128)}, f32[80,640]{1,0:T(8,128)S(1)}, ...), condition=%wide.region_6.7_spmd, body=%wide.region_1.6_spmd.sunk | while | flops 728267520 | bytes 9130165 | solution.py:66
  44.9 29.3 %all-gather.2.cloned.1.call-done = f32[640,640]{1,0:T(8,128)} async-done(((f32[80,640]{1,0:T(8,128)}), f32[640,640]{1,0:T(8,128)}) %all-gather.2.cloned.1.call-update) | async-done | bytes 1638416 | tf_op jit(solution)/shard_map/all_gather | solution.py:69
  74.2 626.8 %while.43 = (s32[]{:T(128)}, f32[640]{0:T(1024)S(1)}, pred[]{:T(512)}, f32[640,640]{1,0:T(8,128)}, f32[640]{0:T(1024)S(1)}, /*index=5*/s32[]{:T(128)}, f32[]{:T(128)}) while((s32[]{:T(128)}, f32[640]{0:T(1024)S(1)}, pred[]{:T(512)}, f32[640,640]{1,0:T(8,128)}, f32[640]{0:T(1024)S(1)}, /*index=5*/s32[]{:T(128)}, f32[]{:T(128)}) %tuple.76), condition=%wide.region_9.10_spmd, body=%wide.region_7.9_spmd.sunk | while | flops 4917121 | bytes 1674370 | solution.py:78
  90.0 4.5 collective-permute-done
  100.0 4.5 collective-permute-done
  119.8 4.5 collective-permute-done
  129.8 4.5 collective-permute-done
  149.7 4.5 collective-permute-done
  169.5 4.5 collective-permute-done
  179.5 4.5 collective-permute-done
  199.4 4.5 collective-permute-done
  209.3 4.5 collective-permute-done
  229.2 4.5 collective-permute-done
  259.0 4.5 collective-permute-done
  278.9 4.5 collective-permute-done
  288.8 4.5 collective-permute-done
  308.7 4.5 collective-permute-done
  318.7 4.5 collective-permute-done
  338.5 4.5 collective-permute-done
  358.4 4.5 collective-permute-done
  368.4 4.5 collective-permute-done
  388.2 4.5 collective-permute-done
  398.2 4.5 collective-permute-done
  418.1 4.5 collective-permute-done
  447.9 4.5 collective-permute-done
  457.8 4.6 collective-permute-done
  477.8 4.5 collective-permute-done
  497.6 4.5 collective-permute-done
  701.0 100.1 %while.44 = (s32[]{:T(128)}, f32[640]{0:T(1024)S(1)}, f32[2,80]{1,0:T(2,128)S(1)}, s32[]{:T(128)}, f32[2,80,640]{2,1,0:T(8,128)S(1)}, /*index=5*/s32[]{:T(128)}, f32[]{:T(128)}, s32[]{:T(128)}) while((s32[]{:T(128)}, f32[640]{0:T(1024)S(1)}, f32[2,80]{1,0:T(2,128)S(1)}, s32[]{:T(128)}, f32[2,80,640]{2,1,0:T(8,128)S(1)}, ...), condition=%wide.region_13.14_spmd, body=%wide.region_10.13_spmd.sunk | while | flops 616401 | bytes 222065 | solution.py:87
  701.3 84.1 %psum.10 = f32[640]{0:T(1024)S(1)} all-reduce(f32[640]{0:T(1024)S(1)} %convolution_reduce_fusion.5), channel_id=1, replica_groups=mesh['tm'=64,'rows'=8] {'rows'}, use_global_device_ids=true, to_apply=%region_11.11 | all-reduce | flops 640 | bytes 5120 | tf_op jit(solution)/shard_map/while/body/eval_jaxpr/psum | solution.py:83
  787.2 12.4 %psum.10 = f32[640]{0:T(1024)S(1)} all-reduce(f32[640]{0:T(1024)S(1)} %convolution_reduce_fusion.5), channel_id=1, replica_groups=mesh['tm'=64,'rows'=8] {'rows'}, use_global_device_ids=true, to_apply=%region_11.11 | all-reduce | flops 640 | bytes 5120 | tf_op jit(solution)/shard_map/while/body/eval_jaxpr/psum | solution.py:83
  (467 shorter events, 541.8 us)
Async XLA Ops:
  6.5 67.7 %all-gather.2.cloned.1.call-start = ((), (), s32[]{:S(2)}) async-start(), calls=%async_computation | async-start | bytes 1843200 | tf_op jit(solution)/shard_map/all_gather | solution.py:69
  7.5 15.2 %collective-permute-start.1 = (f32[64,640]{1,0:T(8,128)S(1)}, f32[64,640]{1,0:T(8,128)S(1)}, u32[]{:S(2)}, u32[]{:S(2)}) collective-permute-start(f32[64,640]{1,0:T(8,128)S(1)} %slice_bitcast_fusion), channel_id=1, source_target_pairs={{0,8},{8,16},{16,24},{24,32},{32,40},{40,48},{48,56},{56,64},{64,7... | collective-permute-start | bytes 491528 | tf_op jit(solution)/shard_map/ppermute | solution.py:10
  77.7 6.9 collective-permute-start
  88.1 6.5 collective-permute-start
  98.0 6.5 collective-permute-start
  117.9 6.5 collective-permute-start
  127.8 6.5 collective-permute-start
  147.7 6.5 collective-permute-start
  167.6 6.5 collective-permute-start
  177.6 6.5 collective-permute-start
  197.4 6.5 collective-permute-start
  207.4 6.5 collective-permute-start
  227.3 6.5 collective-permute-start
  247.1 6.5 collective-permute-start
  257.1 6.5 collective-permute-start
  277.0 6.5 collective-permute-start
  286.9 6.5 collective-permute-start
  306.8 6.5 collective-permute-start
  316.7 6.5 collective-permute-start
  336.6 6.5 collective-permute-start
  356.5 6.5 collective-permute-start
  366.4 6.5 collective-permute-start
  386.3 6.5 collective-permute-start
  396.3 6.5 collective-permute-start
  416.1 6.5 collective-permute-start
  436.0 6.5 collective-permute-start
  446.0 6.5 collective-permute-start
  455.9 6.5 collective-permute-start
  475.8 6.5 collective-permute-start
  495.7 6.5 collective-permute-start
  505.7 6.5 collective-permute-start
  525.5 6.5 collective-permute-start
  (36 other events, 235.3 us)
Sparse Core Ops, SparseCore 0:
  43.6 30.5 all-gather.1
where the time goes:
time: 813 us; the launch traced here: 809 us
  waiting for transfers between devices  326 us (40%)
  matrix products  159 us (20%)
  starting transfers between devices  126 us (15%)
  blocking collectives  96.5 us (12%)
  other arithmetic  77.8 us (10%)
  between operations  13.5 us (2%)
  local copies, waits for them, and re-layouts  8.18 us (1%)
    ppermute x64, waiting for transfers between devices, shifted(): return lax.ppermute(block, axis, route)  296 us
    dot_general x63, matrix products, turn(): jnp.dot(incoming, full_block, precision=highest, preferred_element_type=j...  147 us
    ppermute x64, starting transfers between devices, shifted(): return lax.ppermute(block, axis, route)  126 us
    psum x2, blocking collectives, propagate(): moved = lax.psum(partial_term, 'rows')  96.5 us
    reduce_sum x63, other arithmetic, turn(): moved = moved / jnp.sum(moved)  36.5 us
    div x63, other arithmetic, turn(): moved = moved / jnp.sum(moved)  34.5 us
    all_gather x1, waiting for transfers between devices, shards(): full_block = lax.all_gather(block_part, 'rows', axis=0, tiled=True)  29.3 us
  transfers between devices with their start and end apart: 65, of which 65 were waited for; matrix products, arithmetic and copies ran while one was open for 0% of the time, Pallas kernels for 0%

commit v1 on v0

--- a/solution.py
+++ b/solution.py
@@ -66,7 +66,9 @@
     (block_part, unused), kept_rows = lax.scan(
         accumulate, (block_init, rim), (states, ancestors, tracer_obs, jitter)
     )
-    full_block = lax.all_gather(block_part, "rows", axis=0, tiled=True)
+    full_block = jnp.concatenate(
+        lax.all_to_all(jnp.stack([block_part] * lax.axis_size("rows")), "rows", 0, 0), axis=0
+    )
     start = prior_weights / jnp.sum(prior_weights)
 
     def turn(turn_index, incoming):

time: 813 us -> 723 us (0.89)
  matrix products: 159 us -> 68.5 us
  other arithmetic: 77.8 us -> 93.9 us
  between operations: 13.5 us -> 0.08 us
  waiting for transfers between devices: 326 us -> 317 us
    dot_general x63, matrix products: 147 us -> 56.9 us  [turn(): jnp.dot(incoming, full_block, precision=highest, preferred_element_type=j...]
    all_gather x1 -> x0, waiting for transfers between devices: 29.3 us -> none  [shards(): full_block = lax.all_gather(block_part, 'rows', axis=0, tiled=True)]
    all_to_all x0 -> x1, waiting for transfers between devices: none -> 20 us  [shards(): lax.all_to_all(jnp.stack([block_part] * lax.axis_size('rows')), 'rows', 0...]
    div x63, other arithmetic: 34.5 us -> 43.6 us  [turn(): moved = moved / jnp.sum(moved)]
where the time goes in v1:
time: 723 us; the launch traced here: 719 us
  waiting for transfers between devices  317 us (44%)
  starting transfers between devices  130 us (18%)
  blocking collectives  97.1 us (13%)
  other arithmetic  93.9 us (13%)
  matrix products  68.5 us (9%)
  local copies, waits for them, and re-layouts  8.8 us (1%)
    ppermute x64, waiting for transfers between devices, shifted(): return lax.ppermute(block, axis, route)  297 us
    ppermute x64, starting transfers between devices, shifted(): return lax.ppermute(block, axis, route)  125 us
    psum x2, blocking collectives, propagate(): moved = lax.psum(partial_term, 'rows')  97.1 us
    dot_general x63, matrix products, turn(): jnp.dot(incoming, full_block, precision=highest, preferred_element_type=j...  56.9 us
    div x63, other arithmetic, turn(): moved = moved / jnp.sum(moved)  43.6 us
    reduce_sum x63, other arithmetic, turn(): moved = moved / jnp.sum(moved)  43.5 us
    all_to_all x1, waiting for transfers between devices, shards(): lax.all_to_all(jnp.stack([block_part] * lax.axis_size('rows')), 'rows', 0...  20 us
  transfers between devices with their start and end apart: 65, of which 65 were waited for; matrix products, arithmetic and copies ran while one was open for 0% of the time, Pallas kernels for 0%

profile of v1, /device:TPU:25, one launch (start us, length us, event | category | flops | bytes accessed | tf_op | source)
XLA Modules:
  0.0 718.6 jit_solution(13255250656826157970)
XLA Ops:
  4.6 11.5 %collective-permute-done.1 = f32[64,640]{1,0:T(8,128)S(1)} collective-permute-done((f32[64,640]{1,0:T(8,128)S(1)}, f32[64,640]{1,0:T(8,128)S(1)}, u32[]{:S(2)}, u32[]{:S(2)}) %collective-permute-start.1) | collective-permute-done | bytes 163872 | tf_op jit(solution)/shard_map/ppermute | solution.py:10
  16.2 20.1 %while.42 = (s32[]{:T(128)}, f32[80,640]{1,0:T(8,128)S(1)}, f32[64,640]{1,0:T(8,128)S(1)}, f32[2,80,640]{2,1,0:T(8,128)S(1)}, f32[32]{0:T(128)}, /*index=5*/f32[...) while((s32[]{:T(128)}, f32[80,640]{1,0:T(8,128)S(1)}, ...), condition=%wide.region_6.7_spmd, body=%wide.region_1.6_spmd.sunk | while | flops 728267520 | bytes 9130165 | solution.py:66
  37.6 5.7 all-to-all-start
  44.6 20.0 %all-to-all-done = f32[8,80,640]{2,1,0:T(8,128)S(1)} async-done(((f32[8,80,640]{2,1,0:T(8,128)}), f32[8,80,640]{2,1,0:T(8,128)S(1)}, u32[]{:S(2)}, u32[]{:S(2)}) %all-to-all-start) | async-done | bytes 1638432 | tf_op jit(solution)/shard_map/all_to_all | solution.py:70
  64.6 552.7 %while.43 = (s32[]{:T(128)}, f32[640]{0:T(1024)S(1)}, pred[]{:T(512)}, f32[640,640]{1,0:T(8,128)S(1)}, f32[640]{0:T(1024)S(1)}, /*index=5*/s32[]{:T(128)}, f32[]{:T(128)}) while((s32[]{:T(128)}, f32[640]{0:T(1024)S(1)}, pred[]{:T(512)}, f32[640,640]{1,0:T(8,128)S(1)}, f32[640]{0:T(1024)S(1)}, /*index=5*/s32[]{:T(128)}, f32[]{:T(128)}) %tuple.82), condition=%wide.region_9.10_spmd, body=%wide.region_7.9_spmd.sunk | while | flops 4917121 | bytes 1674370 | solution.py:80
  86.4 4.5 collective-permute-done
  95.2 4.5 collective-permute-done
  103.9 4.5 collective-permute-done
  112.7 4.5 collective-permute-done
  121.5 4.5 collective-permute-done
  165.3 4.5 collective-permute-done
  174.1 4.5 collective-permute-done
  182.8 4.5 collective-permute-done
  191.6 4.5 collective-permute-done
  200.4 4.5 collective-permute-done
  209.1 4.7 collective-permute-done
  253.2 4.5 collective-permute-done
  261.9 4.5 collective-permute-done
  270.7 4.5 collective-permute-done
  279.5 4.5 collective-permute-done
  288.2 4.5 collective-permute-done
  332.1 4.5 collective-permute-done
  340.8 4.5 collective-permute-done
  349.6 4.5 collective-permute-done
  358.4 4.5 collective-permute-done
  367.1 4.6 collective-permute-done
  393.5 4.5 collective-permute-done
  437.3 4.6 collective-permute-done
  595.2 4.6 collective-permute-done
  617.3 100.7 %while.44 = (s32[]{:T(128)}, f32[640]{0:T(1024)S(1)}, f32[2,80]{1,0:T(2,128)S(1)}, s32[]{:T(128)}, f32[2,80,640]{2,1,0:T(8,128)S(1)}, /*index=5*/s32[]{:T(128)}, f32[]{:T(128)}, s32[]{:T(128)}) while((s32[]{:T(128)}, f32[640]{0:T(1024)S(1)}, f32[2,80]{1,0:T(2,128)S(1)}, s32[]{:T(128)}, f32[2,80,640]{2,1,0:T(8,128)S(1)}, ...), condition=%wide.region_13.14_spmd, body=%wide.region_10.13_spmd.sunk | while | flops 616401 | bytes 222065 | solution.py:89
  617.6 84.7 %psum.10 = f32[640]{0:T(1024)S(1)} all-reduce(f32[640]{0:T(1024)S(1)} %convolution_reduce_fusion.5), channel_id=1, replica_groups=mesh['tm'=64,'rows'=8] {'rows'}, use_global_device_ids=true, to_apply=%region_11.11 | all-reduce | flops 640 | bytes 5120 | tf_op jit(solution)/shard_map/while/body/eval_jaxpr/psum | solution.py:85
  704.1 12.4 %psum.10 = f32[640]{0:T(1024)S(1)} all-reduce(f32[640]{0:T(1024)S(1)} %convolution_reduce_fusion.5), channel_id=1, replica_groups=mesh['tm'=64,'rows'=8] {'rows'}, use_global_device_ids=true, to_apply=%region_11.11 | all-reduce | flops 640 | bytes 5120 | tf_op jit(solution)/shard_map/while/body/eval_jaxpr/psum | solution.py:85
  (465 shorter events, 472.5 us)
Async XLA Ops:
  0.9 15.2 %collective-permute-start.1 = (f32[64,640]{1,0:T(8,128)S(1)}, f32[64,640]{1,0:T(8,128)S(1)}, u32[]{:S(2)}, u32[]{:S(2)}) collective-permute-start(f32[64,640]{1,0:T(8,128)S(1)} %slice_bitcast_fusion), channel_id=1, source_target_pairs={{0,8},{8,16},{16,24},{24,32},{32,40},{40,48},{48,56},{56,64},{64,7... | collective-permute-start | bytes 491528 | tf_op jit(solution)/shard_map/ppermute | solution.py:10
  37.6 27.1 %all-to-all-start = ((f32[8,80,640]{2,1,0:T(8,128)}), f32[8,80,640]{2,1,0:T(8,128)S(1)}, u32[]{:S(2)}, u32[]{:S(2)}) async-start(f32[8,80,640]{2,1,0:T(8,128)} %stack.2), calls=%async_computation | async-start | bytes 3276800 | tf_op jit(solution)/shard_map/all_to_all | solution.py:70
  84.5 6.5 collective-permute-start
  93.2 6.5 collective-permute-start
  102.0 6.5 collective-permute-start
  110.8 6.5 collective-permute-start
  119.5 6.5 collective-permute-start
  128.3 6.5 collective-permute-start
  163.4 6.5 collective-permute-start
  172.1 6.5 collective-permute-start
  180.9 6.5 collective-permute-start
  189.7 6.5 collective-permute-start
  198.4 6.5 collective-permute-start
  207.2 6.7 collective-permute-start
  251.2 6.5 collective-permute-start
  260.0 6.5 collective-permute-start
  268.8 6.5 collective-permute-start
  277.5 6.5 collective-permute-start
  286.3 6.5 collective-permute-start
  295.1 6.5 collective-permute-start
  330.1 6.5 collective-permute-start
  338.9 6.5 collective-permute-start
  347.7 6.5 collective-permute-start
  356.4 6.5 collective-permute-start
  365.2 6.5 collective-permute-start
  391.5 6.5 collective-permute-start
  400.3 6.5 collective-permute-start
  409.1 6.5 collective-permute-start
  417.8 6.5 collective-permute-start
  426.6 6.5 collective-permute-start
  435.4 6.6 collective-permute-start
  593.3 6.5 collective-permute-start
  (35 other events, 219.4 us)
